TPU v7x, 32 devices: a whole 2x2x4 slice. The times are simulated.
32 devices in a mesh: dp: 2 (over y), fsdp: 16 (over z, x, core).
Axes of the slice: x: 2, y: 2, z: 4, core: 2. Of those that a mesh axis runs over, the one named last changes fastest.
Arguments:
- tokens: bfloat16 [64, 512, 768], P(('dp', 'fsdp')), may hold values from -6 to 6
- out_grad: bfloat16 [64, 512, 768], P(('dp', 'fsdp')), may hold values from -6 to 6
- lengths: int32 [64], P(('dp', 'fsdp')), may hold values from 128 to 512, as said below
- labels: int32 [64], P(('dp', 'fsdp')), may hold values from 0 to 2
- exit_layers: int32 [64], P(('dp', 'fsdp')), may hold values from 0 to 11, as said below
- mat_master: float32 [9984, 768], P('fsdp')
- mat_first: float32 [9984, 768], P('fsdp')
- mat_second: float32 [9984, 768], P('fsdp'), as said below
- vec_master: float32 [16, 768], P(None, 'fsdp')
- vec_first: float32 [16, 768], P(None, 'fsdp')
- vec_second: float32 [16, 768], P(None, 'fsdp'), as said below
- cls_bias: float32 [3], replicated, may hold values from -3 to 3
- cls_first: float32 [3], replicated
- cls_second: float32 [3], replicated, as said below
Outputs:
- block_out: bfloat16 [64, 512, 768], P(('dp', 'fsdp'))
- input_grad: bfloat16 [64, 512, 768], P(('dp', 'fsdp'))
- ramp_loss: float32 [], replicated
- mat_master_new: float32 [9984, 768], P('fsdp')
- mat_first_new: float32 [9984, 768], P('fsdp')
- mat_second_new: float32 [9984, 768], P('fsdp')
- mat_copy: bfloat16 [9984, 768], P('fsdp')
- vec_master_new: float32 [16, 768], P(None, 'fsdp')
- vec_first_new: float32 [16, 768], P(None, 'fsdp')
- vec_second_new: float32 [16, 768], P(None, 'fsdp')
- vec_copy: bfloat16 [16, 768], P(None, 'fsdp')
- cls_bias_new: float32 [3], replicated
- cls_first_new: float32 [3], replicated
- cls_second_new: float32 [3], replicated
Inputs may be any that keep to these rules, and one draw needn't show every extreme that they name: Keys at positions of lengths or later are padding; some sequence has 512 tokens and some 512 // 4. `exit_layers`: a sequence whose exit layer is below 6 has left the encoder and is out of the loss; some sequence exits at layer 0 and some at the last. `mat_second`: positive. `vec_second`: positive. `cls_second`: positive.
All inputs are finite; a program needn't handle non-finite values.
Results may differ from a plain program's by a relative error of at most 0.02.
Values may be sent and summed in bfloat16 or wider, within the bound.
No kernel may reach another device: no remote copies, remote signals or barrier semaphores. Data moves between devices by JAX's collectives and lax.ppermute only.
A program may use at most 192 MiB of HBM per device.

v0:
```python
import jax
import jax.numpy as jnp
from jax import lax
from jax.sharding import PartitionSpec as P

D = 768
H = 12
HD = 64
FF = 3072
LAYER = 6
NCLS = 3
L = 512
STEP = 10
BETA_ONE = 0.9
BETA_TWO = 0.999
ADAM_EPS = 1e-08
WEIGHT_DECAY = 0.01
LN_EPS = 1e-12
VEC_RATE = 0.5
MASK_FILL = -1000000000.0


def product(first_arg, second_arg):
    return jnp.dot(first_arg, second_arg, preferred_element_type=jnp.float32)


def product_last(first_arg, second_arg):
    return lax.dot_general(
        first_arg, second_arg, (((1,), (1,)), ((), ())), preferred_element_type=jnp.float32
    )


def product_first(first_arg, second_arg):
    return lax.dot_general(
        first_arg, second_arg, (((0,), (0,)), ((), ())), preferred_element_type=jnp.float32
    )


def norm_forward(hidden, gain_vec, shift_vec):
    centre = jnp.mean(hidden, axis=-1, keepdims=True)
    centred = hidden - centre
    spread = jnp.mean(centred * centred, axis=-1, keepdims=True)
    inv_dev = lax.rsqrt(spread + LN_EPS)
    normed = centred * inv_dev
    return (normed * gain_vec + shift_vec, normed, inv_dev)


def norm_backward(grad_in, normed, inv_dev, gain_vec):
    scaled = grad_in * gain_vec
    return inv_dev * (
        scaled
        - jnp.mean(scaled, axis=-1, keepdims=True)
        - normed * jnp.mean(scaled * normed, axis=-1, keepdims=True)
    )


def split_matrices(matrices):
    return (
        matrices[0:D],
        matrices[D : 2 * D],
        matrices[2 * D : 3 * D],
        matrices[3 * D : 4 * D],
        matrices[4 * D : 5 * D],
        matrices[5 * D : 5 * D + FF],
        matrices[5 * D + FF : 5 * D + 2 * FF],
    )


def split_vectors(vectors):
    inner_rows = FF // D
    values_f = vectors.astype(jnp.float32)
    return (
        values_f[0],
        values_f[1],
        values_f[2],
        values_f[3],
        values_f[4],
        values_f[5],
        values_f[6],
        values_f[7],
        values_f[8],
        values_f[9 : 9 + inner_rows].reshape(FF),
        vectors[9 + inner_rows : 9 + inner_rows + NCLS],
    )


def row_rates(row_index):
    base_rate = D ** (-0.5)
    return jnp.where(
        (row_index >= 3 * D) & (row_index < 4 * D),
        8.0 * base_rate,
        jnp.where(row_index >= 5 * D + FF, 1.5 * FF ** (-0.5), base_rate),
    )


def adam_update(master, first_mom, second_mom, grad_in, rate, decay):
    first_new = BETA_ONE * first_mom + (1.0 - BETA_ONE) * grad_in
    second_new = BETA_TWO * second_mom + (1.0 - BETA_TWO) * grad_in * grad_in
    fix_one = 1.0 - BETA_ONE**STEP
    fix_two = 1.0 - BETA_TWO**STEP
    direction = first_new / fix_one / (jnp.sqrt(second_new / fix_two) + ADAM_EPS)
    master_new = master - rate * (direction + decay * master)
    return (master_new, first_new, second_new)


def masked_scores(q_seq, k_seq, length):
    score_scale = HD ** (-0.5)
    scores = (
        jnp.einsum("qhd,khd->hqk", q_seq, k_seq, preferred_element_type=jnp.float32) * score_scale
    )
    key_valid = jnp.arange(q_seq.shape[0]) < length
    return jnp.where(key_valid[None, None, :], scores, MASK_FILL)


def attend(seq_parts):
    q_seq, k_seq, v_seq, length = seq_parts
    scores = masked_scores(q_seq, k_seq, length)
    row_max = jnp.max(scores, axis=-1, keepdims=True)
    exp_scores = jnp.exp(scores - row_max)
    exp_total = jnp.sum(exp_scores, axis=-1, keepdims=True)
    attn_probs = exp_scores / exp_total
    log_total = row_max + jnp.log(exp_total)
    context = jnp.einsum(
        "hqk,khd->qhd", attn_probs.astype(jnp.bfloat16), v_seq, preferred_element_type=jnp.float32
    )
    return (context.astype(jnp.bfloat16), log_total)


def attend_back(seq_parts):
    q_seq, k_seq, v_seq, length, log_total, grad_ctx = seq_parts
    score_scale = HD ** (-0.5)
    attn_probs = jnp.exp(masked_scores(q_seq, k_seq, length) - log_total)
    grad_probs = jnp.einsum("qhd,khd->hqk", grad_ctx, v_seq, preferred_element_type=jnp.float32)
    grad_values = jnp.einsum(
        "hqk,qhd->khd",
        attn_probs.astype(jnp.bfloat16),
        grad_ctx,
        preferred_element_type=jnp.float32,
    )
    grad_scores = attn_probs * (
        grad_probs - jnp.sum(attn_probs * grad_probs, axis=-1, keepdims=True)
    )
    rounded = grad_scores.astype(jnp.bfloat16)
    grad_query = (
        jnp.einsum("hqk,khd->qhd", rounded, k_seq, preferred_element_type=jnp.float32) * score_scale
    )
    grad_keys = (
        jnp.einsum("hqk,qhd->khd", rounded, q_seq, preferred_element_type=jnp.float32) * score_scale
    )
    return (
        grad_query.astype(jnp.bfloat16),
        grad_keys.astype(jnp.bfloat16),
        grad_values.astype(jnp.bfloat16),
    )


def on_device(
    tokens,
    out_grad,
    lengths,
    labels,
    exit_layers,
    mat_master,
    mat_first,
    mat_second,
    vec_master,
    vec_first,
    vec_second,
    cls_bias,
    cls_first,
    cls_second,
):
    seq_count = tokens.shape[0]
    tok_count = seq_count * L
    active = (exit_layers >= LAYER).astype(jnp.float32)
    mat_low = mat_master.astype(jnp.bfloat16)
    vec_low = vec_master.astype(jnp.bfloat16)
    matrices, vectors = (
        lax.all_gather(mat_low, "fsdp", axis=0, tiled=True),
        lax.all_gather(vec_low, "fsdp", axis=1, tiled=True),
    )
    w_query, w_key, w_value, w_out, w_pool, w_inner, w_outer = split_matrices(matrices)
    (
        b_query,
        b_value,
        b_out,
        gain_one,
        shift_one,
        b_outer,
        gain_two,
        shift_two,
        b_pool,
        b_inner,
        w_class,
    ) = split_vectors(vectors)
    token_rows = tokens.reshape(tok_count, D)
    query_rows = (product(token_rows, w_query) + b_query).astype(jnp.bfloat16)
    key_rows = product(token_rows, w_key).astype(jnp.bfloat16)
    value_rows = (product(token_rows, w_value) + b_value).astype(jnp.bfloat16)
    q_heads = query_rows.reshape(seq_count, L, H, HD)
    k_heads = key_rows.reshape(seq_count, L, H, HD)
    v_heads = value_rows.reshape(seq_count, L, H, HD)
    context, log_total = lax.map(attend, (q_heads, k_heads, v_heads, lengths))
    ctx_rows = context.reshape(tok_count, D)
    resid_attn = token_rows.astype(jnp.float32) + (product(ctx_rows, w_out) + b_out)
    normed_out, normed_one, inv_one = norm_forward(resid_attn, gain_one, shift_one)
    normed_low = normed_out.astype(jnp.bfloat16)
    inner_pre = product_last(normed_low, w_inner) + b_inner
    activated = jax.nn.gelu(inner_pre, approximate=False).astype(jnp.bfloat16)
    resid_ffn = normed_out + (product(activated, w_outer) + b_outer)
    layer_out, normed_two, inv_two = norm_forward(resid_ffn, gain_two, shift_two)
    block_out = layer_out.astype(jnp.bfloat16).reshape(seq_count, L, D)
    first_row = block_out[:, 0, :]
    pooled = jnp.tanh(product(first_row, w_pool) + b_pool)
    pooled_low = pooled.astype(jnp.bfloat16)
    logits = product_last(pooled_low, w_class) + cls_bias
    log_norm = jax.nn.logsumexp(logits, axis=-1)
    onehot = (labels[:, None] == jnp.arange(NCLS)[None, :]).astype(jnp.float32)
    cross_ent = log_norm - jnp.sum(logits * onehot, axis=-1)
    ce_sum = jnp.sum(active * cross_ent)
    class_error = active[:, None] * (jnp.exp(logits - log_norm[:, None]) - onehot)
    error_sum = jnp.sum(class_error, axis=0)
    ce_total, active_count, error_total = lax.psum(
        (ce_sum, jnp.sum(active), error_sum), ("dp", "fsdp")
    )
    matrices, vectors = (
        lax.all_gather(mat_low, "fsdp", axis=0, tiled=True),
        lax.all_gather(vec_low, "fsdp", axis=1, tiled=True),
    )
    w_query, w_key, w_value, w_out, w_pool, w_inner, w_outer = split_matrices(matrices)
    (
        b_query,
        b_value,
        b_out,
        gain_one,
        shift_one,
        b_outer,
        gain_two,
        shift_two,
        b_pool,
        b_inner,
        w_class,
    ) = split_vectors(vectors)
    grad_logit = (class_error / active_count).astype(jnp.bfloat16)
    grad_pool = product(grad_logit, w_class)
    grad_pre = (grad_pool * (1.0 - pooled * pooled)).astype(jnp.bfloat16)
    grad_b_pool = jnp.sum(grad_pre.astype(jnp.float32), axis=0)
    grad_w_pool = product_first(first_row, grad_pre)
    grad_w_class = product_first(grad_logit, pooled_low)
    grad_first = product_last(grad_pre, w_pool)
    grad_layer = out_grad.astype(jnp.float32).at[:, 0, :].add(grad_first).reshape(tok_count, D)
    grad_gain_two = jnp.sum(grad_layer * normed_two, axis=0)
    grad_shift_two = jnp.sum(grad_layer, axis=0)
    grad_resid_ffn = norm_backward(grad_layer, normed_two, inv_two, gain_two)
    grad_ffn = grad_resid_ffn.astype(jnp.bfloat16)
    grad_b_outer = jnp.sum(grad_ffn.astype(jnp.float32), axis=0)
    inner_again = product_last(normed_low, w_inner) + b_inner
    gelu_out, gelu_pull = jax.vjp(
        lambda inner_val: jax.nn.gelu(inner_val, approximate=False), inner_again
    )
    activ_again = gelu_out.astype(jnp.bfloat16)
    grad_w_outer = product_first(activ_again, grad_ffn)
    grad_activ = product_last(grad_ffn, w_outer)
    grad_inner = gelu_pull(grad_activ)[0].astype(jnp.bfloat16)
    grad_b_inner = jnp.sum(grad_inner.astype(jnp.float32), axis=0)
    grad_w_inner = product_first(grad_inner, normed_low)
    grad_normed = grad_resid_ffn + product(grad_inner, w_inner)
    grad_gain_one = jnp.sum(grad_normed * normed_one, axis=0)
    grad_shift_one = jnp.sum(grad_normed, axis=0)
    grad_resid_attn = norm_backward(grad_normed, normed_one, inv_one, gain_one)
    grad_attn = grad_resid_attn.astype(jnp.bfloat16)
    grad_b_out = jnp.sum(grad_attn.astype(jnp.float32), axis=0)
    grad_w_out = product_first(ctx_rows, grad_attn)
    grad_ctx = product_last(grad_attn, w_out).astype(jnp.bfloat16).reshape(seq_count, L, H, HD)
    grad_q, grad_k, grad_v = lax.map(
        attend_back, (q_heads, k_heads, v_heads, lengths, log_total, grad_ctx)
    )
    grad_q = grad_q.reshape(tok_count, D)
    grad_k = grad_k.reshape(tok_count, D)
    grad_v = grad_v.reshape(tok_count, D)
    grad_b_query = jnp.sum(grad_q.astype(jnp.float32), axis=0)
    grad_b_value = jnp.sum(grad_v.astype(jnp.float32), axis=0)
    grad_w_query = product_first(token_rows, grad_q)
    grad_w_key = product_first(token_rows, grad_k)
    grad_w_value = product_first(token_rows, grad_v)
    grad_tokens = (
        grad_resid_attn
        + product_last(grad_q, w_query)
        + product_last(grad_k, w_key)
        + product_last(grad_v, w_value)
    )
    input_grad = grad_tokens.astype(jnp.bfloat16).reshape(seq_count, L, D)
    mat_grad = jnp.concatenate(
        [
            grad_w_query,
            grad_w_key,
            grad_w_value,
            grad_w_out,
            grad_w_pool,
            grad_w_inner,
            grad_w_outer,
        ],
        axis=0,
    )
    head_rows = jnp.stack(
        [
            grad_b_query,
            grad_b_value,
            grad_b_out,
            grad_gain_one,
            grad_shift_one,
            grad_b_outer,
            grad_gain_two,
            grad_shift_two,
            grad_b_pool,
        ],
        axis=0,
    )
    vec_grad = jnp.concatenate([head_rows, grad_b_inner.reshape(FF // D, D), grad_w_class], axis=0)
    mat_part, vec_part = (
        lax.psum_scatter(
            mat_grad.astype(jnp.bfloat16), "fsdp", scatter_dimension=0, tiled=True
        ).astype(jnp.float32),
        lax.psum_scatter(
            vec_grad.astype(jnp.bfloat16), "fsdp", scatter_dimension=1, tiled=True
        ).astype(jnp.float32),
    )
    mat_total, vec_total = (
        lax.psum(mat_part.astype(jnp.bfloat16), "dp").astype(jnp.float32),
        lax.psum(vec_part.astype(jnp.bfloat16), "dp").astype(jnp.float32),
    )
    ramp_loss = ce_total / active_count
    cls_grad = error_total / active_count
    shard_rows = mat_master.shape[0]
    row_index = lax.axis_index("fsdp") * shard_rows + jnp.arange(shard_rows)
    rates = row_rates(row_index)[:, None]
    mat_new, mat_first_new, mat_second_new = adam_update(
        mat_master, mat_first, mat_second, mat_total, rates, WEIGHT_DECAY
    )
    vec_new, vec_first_new, vec_second_new = adam_update(
        vec_master, vec_first, vec_second, vec_total, VEC_RATE, 0.0
    )
    cls_new, cls_first_new, cls_second_new = adam_update(
        cls_bias, cls_first, cls_second, cls_grad, VEC_RATE, 0.0
    )
    return (
        block_out,
        input_grad,
        ramp_loss,
        mat_new,
        mat_first_new,
        mat_second_new,
        mat_new.astype(jnp.bfloat16),
        vec_new,
        vec_first_new,
        vec_second_new,
        vec_new.astype(jnp.bfloat16),
        cls_new,
        cls_first_new,
        cls_second_new,
    )


def solution(mesh):
    placed = (
        P(("dp", "fsdp"), None, None),
        P(("dp", "fsdp"), None, None),
        P(("dp", "fsdp")),
        P(("dp", "fsdp")),
        P(("dp", "fsdp")),
        P("fsdp", None),
        P("fsdp", None),
        P("fsdp", None),
        P(None, "fsdp"),
        P(None, "fsdp"),
        P(None, "fsdp"),
        P(),
        P(),
        P(),
    )
    return jax.shard_map(
        on_device,
        mesh=mesh,
        in_specs=placed,
        out_specs=(
            P(("dp", "fsdp"), None, None),
            P(("dp", "fsdp"), None, None),
            P(),
            P("fsdp", None),
            P("fsdp", None),
            P("fsdp", None),
            P("fsdp", None),
            P(None, "fsdp"),
            P(None, "fsdp"),
            P(None, "fsdp"),
            P(None, "fsdp"),
            P(),
            P(),
            P(),
        ),
        check_vma=False,
    )
```

profile of v0, /device:TPU:0, one launch (start us, length us, event | category | flops | bytes accessed | tf_op | source)
XLA Modules:
  0.0 690.1 jit_solution(1368104361643564995)
XLA Ops:
  7.3 2.7 convert_element_type.137
  10.0 23.6 %all-gather = bf16[16,48,16]{1,2,0:T(8,128)(2,1)S(1)} all-gather(bf16[1,48,16]{1,2,0:T(8,128)(2,1)S(1)} %convert_bitcast_fusion), channel_id=1, replica_groups=mesh['dp'=2,'fsdp'=16] {'fsdp'}, dimensions={0}, use_global_device_ids=true | all-gather | bytes 26112 | tf_op jit(solution)/shard_map/all_gather | solution.py:180
  35.0 3.2 copy_convert_fusion
  38.3 93.3 %all-gather.3.cloned.1.call-done = bf16[9984,768]{1,0:T(8,128)(2,1)} async-done(((bf16[624,768]{1,0:T(8,128)(2,1)}), bf16[9984,768]{1,0:T(8,128)(2,1)}) %all-gather.3.cloned.1.call-update) | async-done | bytes 15335440 | tf_op jit(solution)/shard_map/all_gather | solution.py:179
  131.6 3.1 add_convert_fusion.4
  136.7 1.5 copy.116
  138.4 2.7 add_convert_fusion.3
  144.5 3.8 convolution_convert_fusion.3
  148.3 1.7 copy.115
  150.0 2.4 reshape.216
  152.4 1.7 copy.118
  155.4 22.9 %while.27 = (s32[]{:T(128)}, bf16[2,512,12,64]{1,3,2,0:T(8,128)(2,1)}, f32[2,12,512,1]{2,1,3,0:T(8,128)S(1)}, bf16[2,512,12,64]{1,3,2,0:T(8,128)(2,1)}, s32[2]{0...) while((s32[]{:T(128)}, ...), condition=%wide.region_3.4_spmd, body=%wide.region_0.3_spmd.sunk | while | flops 843442688 | bytes 47427716 | solution.py:203
  157.1 3.1 fusion.182
  160.2 2.6 fusion.183
  162.9 4.2 fusion.184
  168.3 3.1 fusion.182
  171.4 2.6 fusion.183
  174.0 4.2 fusion.184
  178.4 4.2 copy.119
  183.1 3.5 fusion.138
  187.1 36.7 %multiply_convert_fusion.3 = (bf16[1024,3072]{1,0:T(8,128)(2,1)S(1)}, f32[1024,3072]{1,0:T(8,128)}, f32[1024,3072]{1,0:T(8,128)}) fusion(f32[3072]{0:T(1024)S(1)} %add.241, bf16[9984,768]{1,0:T(8,128)(2,1)} %all-gather.3.cloned.1.call-done, f32[1024,768]{1,0:T(8,128)S(1)} %get-tuple-element.291, f32[768]{0:T(1024)S(1)} %get-tuple-element.220, ...), kind=kOutput, calls=%fused_computation.65 | convolution fusion | flops 5043388416 | bytes 39348224 | tf_op jit(solution)/shard_map/dot_general | solution.py:28
  223.9 9.9 %fusion.139 = (f32[1024]{0:T(1024)S(1)}, f32[1024,768]{1,0:T(8,128)S(1)}) fusion(f32[768]{0:T(1024)S(1)} %copy-done.61, bf16[1024,3072]{1,0:T(8,128)(2,1)S(1)} %get-tuple-element.284, bf16[9984,768]{1,0:T(8,128)(2,1)} %all-gather.3.cloned.1.call-done, f32[768]{0:T(1024)S(1)} %get-tuple-element.220, f32[768]{0:T(1024)S(1)} %get-tuple-element.221, ...), kind=kOutput, calls=%fused_computation.220 | convolution fusion | flops 4837342208 | bytes 17323008 | tf_op jit(solution)/shard_map/dot_general | solution.py:24
  236.2 1.5 fusion.91
  239.0 39.1 %all-reduce = (f32[]{:T(128)}, f32[]{:T(128)}, f32[3]{0:T(128)}) all-reduce(f32[]{:T(128)} %get-tuple-element.228, f32[]{:T(128)} %get-tuple-element.227, f32[3]{0:T(128)S(1)} %get-tuple-element.281), channel_id=1, replica_groups=mesh['dp'=2,'fsdp'=16] {'dp','fsdp'}, use_global_device_ids=true, to_apply=%region_11.12 | all-reduce | flops 5 | bytes 40 | tf_op jit(solution)/shard_map/psum | solution.py:223
  279.5 2.3 fusion.90
  281.8 2.3 copy.121
  284.7 2.6 fusion.128
  287.3 1.7 fusion.72
  289.1 4.3 convert_reduce_fusion.1
  293.4 19.4 %fusion.142 = (bf16[3072]{0:T(1024)(128)(2,1)}, bf16[1024,3072]{1,0:T(8,128)(2,1)}) fusion(f32[1024,3072]{1,0:T(8,128)} %get-tuple-element.285, bf16[9984,768]{1,0:T(8,128)(2,1)} %all-gather.3.cloned.1.call-done, f32[1024,768]{1,0:T(8,128)} %get-tuple-element.274, f32[1024,3072]{1,0:T(8,128)} %get-tuple-element.292, f32[3072]{0:T(1024)S(1)} %add.241), kind=kOutput, calls=%fused_computation.223 | convolution fusion | flops 4882953216 | bytes 39340032 | tf_op jit(solution)/shard_map/dot_general | solution.py:28
  312.8 10.5 %multiply_reduce_fusion.1 = (bf16[768]{0:T(1024)(128)(2,1)}, f32[1024]{0:T(1024)S(1)}, f32[1024]{0:T(1024)S(1)}, bf16[768]{0:T(1024)(128)(2,1)}, f32[1024,768]{1,0:T(8,128)S(1)}) fusion(f32[1024,768]{1,0:T(8,128)S(1)} %copy-done.14, f32[1024]{0:T(1024)S(1)} %add_rsqrt_fusion.1, f32[1024]{0:T(1024)S(1)} %broadcast_multiply_fusion.5, ...), kind=kOutput, calls=%fused_computation.93 | convolution fusion | flops 4839698432 | bytes 20469760 | tf_op jit(solution)/shard_map/dot_general | solution.py:24
  323.2 1.9 convert_reduce_fusion
  325.1 1.6 copy-done.16
  326.7 2.7 convolution_convert_fusion.2
  331.4 1.5 copy.126
  336.9 52.1 %while.28 = (s32[]{:T(128)}, bf16[2,512,12,64]{1,3,2,0:T(8,128)(2,1)}, bf16[2,512,12,64]{1,3,2,0:T(8,128)(2,1)}, bf16[2,512,12,64]{1,3,2,0:T(8,128)(2,1)}, bf16[...) while((s32[]{:T(128)}, ...), condition=%wide.region_18.19_spmd, body=%wide.region_16.18_spmd.sunk | while | flops 2062412288 | bytes 140180784 | solution.py:275
  336.9 1.8 fusion.193
  340.0 7.3 %multiply_reduce_fusion.9 = (f32[12,512]{1,0:T(8,128)S(1)}, f32[12,512,512]{1,2,0:T(8,128)}) fusion(f32[12,512,512]{1,2,0:T(8,128)S(1)} %fusion.193, f32[12,512]{1,0:T(8,128)S(1)} %dynamic-slice_bitcast_fusion.2, pred[512]{0:T(512)(128)(4,1)S(1)} %iota_compare_fusion.6, bf16[2,512,12,64]{1,3,2,0:T(8,128)(2,1)S(1)} %copy-done.7, ...), kind=kOutput, calls=%fused_computation.23.clone.1 | convolution fusion | flops 418375680 | bytes 26797568 | tf_op jit(solution)/shard_map/while/body/eval_jaxpr/qhd,khd->hqk/dot_general | solution.py:133
  347.4 7.2 %multiply_convert_fusion.5 = bf16[12,512,512]{1,2,0:T(8,128)(2,1)S(1)} fusion(f32[12,512,512]{1,2,0:T(8,128)} %get-tuple-element.414, f32[12,512,512]{1,2,0:T(8,128)S(1)} %fusion.193, f32[12,512]{1,0:T(8,128)S(1)} %get-tuple-element.415, f32[12,512]{1,0:T(8,128)S(1)} %dynamic-slice_bitcast_fusion.2, pred[512]{0:T(512)(128)(4,1)S(1)} %iota_compare_fusion.6), kind=kLoop, calls=%fused_computation.22.clone.1 | loop fusion | flops 18874368 | bytes 31506944 | tf_op jit(solution)/shard_map/while/body/eval_jaxpr/convert_element_type | solution.py:143
  354.6 2.0 fusion.195
  358.9 3.8 fusion.196
  362.7 1.8 fusion.193
  365.9 7.3 %multiply_reduce_fusion.9 = (f32[12,512]{1,0:T(8,128)S(1)}, f32[12,512,512]{1,2,0:T(8,128)}) fusion(f32[12,512,512]{1,2,0:T(8,128)S(1)} %fusion.193, f32[12,512]{1,0:T(8,128)S(1)} %dynamic-slice_bitcast_fusion.2, pred[512]{0:T(512)(128)(4,1)S(1)} %iota_compare_fusion.6, bf16[2,512,12,64]{1,3,2,0:T(8,128)(2,1)S(1)} %copy-done.7, ...), kind=kOutput, calls=%fused_computation.23.clone.1 | convolution fusion | flops 418375680 | bytes 26797568 | tf_op jit(solution)/shard_map/while/body/eval_jaxpr/qhd,khd->hqk/dot_general | solution.py:133
  373.2 7.2 %multiply_convert_fusion.5 = bf16[12,512,512]{1,2,0:T(8,128)(2,1)S(1)} fusion(f32[12,512,512]{1,2,0:T(8,128)} %get-tuple-element.414, f32[12,512,512]{1,2,0:T(8,128)S(1)} %fusion.193, f32[12,512]{1,0:T(8,128)S(1)} %get-tuple-element.415, f32[12,512]{1,0:T(8,128)S(1)} %dynamic-slice_bitcast_fusion.2, pred[512]{0:T(512)(128)(4,1)S(1)} %iota_compare_fusion.6), kind=kLoop, calls=%fused_computation.22.clone.1 | loop fusion | flops 18874368 | bytes 31506944 | tf_op jit(solution)/shard_map/while/body/eval_jaxpr/convert_element_type | solution.py:143
  380.4 2.0 fusion.195
  384.8 3.8 fusion.196
  388.9 3.1 copy.128
  392.5 2.5 fusion.84
  395.1 1.6 copy.129
  397.2 1.6 copy.130
  399.2 2.5 fusion.86
  401.7 2.5 fusion.88
  404.3 2.4 fusion.82
  406.8 1.7 fusion.81
  408.5 7.8 %fusion.64 = bf16[9984,768]{1,0:T(8,128)(2,1)} fusion(bf16[9984,768]{1,0:T(8,128)(2,1)} %fusion.81, bf16[1024,3072]{1,0:T(8,128)(2,1)S(1)} %bitcast.232, f32[1024,768]{1,0:T(8,128)S(1)} %copy-done.15, f32[768]{0:T(1024)S(1)} %copy-done.60, f32[768]{0:T(1024)S(1)} %copy-done.43, f32[1024]{0:T(1024)S(1)} %copy-done.45, f32[1024]{0:T(1024)S(1)} %copy-done.37), kind=kOutput, calls=%fused_computation.82 | convolution fusion | flops 4838129664 | bytes 14170112 | tf_op jit(solution)/shard_map/dot_general | solution.py:34
  416.4 7.1 %fusion.63 = bf16[9984,768]{1,0:T(8,128)(2,1)} fusion(bf16[9984,768]{1,0:T(8,128)(2,1)} %fusion.64, bf16[1024,3072]{1,0:T(8,128)(2,1)S(1)} %bitcast.234, f32[1024,768]{1,0:T(8,128)S(1)} %copy-done.23), kind=kOutput, calls=%fused_computation.80 | convolution fusion | flops 4834983936 | bytes 14155776 | tf_op jit(solution)/shard_map/dot_general | solution.py:34
  427.7 5.0 fusion.100
  432.6 4.8 fusion.97
  437.4 141.5 %reduce-scatter.5.cloned.1.call-done = bf16[624,768]{1,0:T(8,128)(2,1)} async-done(((bf16[9984,768]{1,0:T(8,128)(2,1)}), bf16[624,768]{1,0:T(8,128)(2,1)}) %reduce-scatter.5.cloned.1.call-update) | async-done | bytes 958480 | tf_op jit(solution)/shard_map/reduce_scatter | solution.py:321
  581.6 6.3 add_convert_fusion.1
  588.0 47.8 %reduce-scatter.7.cloned.1.call-done = bf16[48,16]{1,0:T(8,128)(2,1)} async-done(((bf16[768,16]{1,0:T(8,128)(2,1)}), bf16[48,16]{1,0:T(8,128)(2,1)}) %reduce-scatter.7.cloned.1.call-update) | async-done | bytes 1552
  636.6 4.9 psum.38
  642.2 33.0 %all-reduce.3.cloned.1.call-done = bf16[624,768]{1,0:T(8,128)(2,1)} async-done(((bf16[624,768]{1,0:T(8,128)(2,1)}), bf16[624,768]{1,0:T(8,128)(2,1)}) %all-reduce.3.cloned.1.call-update) | async-done | bytes 958480 | tf_op jit(solution)/shard_map/psum | solution.py:329
  675.1 7.2 %fusion.133 = (bf16[624,768]{1,0:T(8,128)(2,1)}, f32[624,768]{1,0:T(8,128)}, f32[624,768]{1,0:T(8,128)}, f32[624,768]{1,0:T(8,128)}) fusion(f32[624,768]{1,0:T(8,128)} %param.25, f32[624]{0:T(1024)S(1)} %select_select_fusion, bf16[624,768]{1,0:T(8,128)(2,1)} %all-reduce.3.cloned.1.call-done, f32[624,768]{1,0:T(8,128)} %param.26, f32[624,768]{1,0:T(8,128)} %param.27), kind=kLoop, calls=%fused_computation.217 | loop fusion | flops 8146944 | bytes 13420992 | tf_op jit(solution)/shard_map/convert_element_type | solution.py:353
  (273 shorter events, 38.1 us)
Async XLA Ops:
  7.2 2.8 copy-start.38
  7.2 27.3 %copy-start.68 = (s32[2]{0:T(128)S(1)}, s32[2]{0:T(128)}, u32[]{:S(2)}) copy-start(s32[2]{0:T(128)} %param.24) | copy-start | bytes 28
  7.2 27.8 %copy-start.30 = (bf16[2,512,768]{2,1,0:T(8,128)(2,1)S(1)}, bf16[2,512,768]{2,1,0:T(8,128)(2,1)}, u32[]{:S(2)}) copy-start(bf16[2,512,768]{2,1,0:T(8,128)(2,1)} %param.21) | copy-start | bytes 4718596
  7.2 124.4 %all-gather.3.cloned.1.call-start = ((), (), s32[]{:S(2)}) async-start(), calls=%async_computation.2 | async-start | bytes 16293888 | tf_op jit(solution)/shard_map/all_gather | solution.py:179
  10.0 569.0 %reduce-scatter.5.cloned.1.call-start = ((), (), s32[]{:S(2)}) async-start(), calls=%async_computation.3 | async-start | bytes 16293888 | tf_op jit(solution)/shard_map/reduce_scatter | solution.py:321
  33.8 97.8 %copy-start.34 = (bf16[768,16]{0,1:T(8,128)(2,1)}, bf16[768,16]{0,1:T(8,128)(2,1)S(1)}, u32[]{:S(2)}) copy-start(bf16[768,16]{0,1:T(8,128)(2,1)S(1)} %reshape.228) | copy-start | bytes 73732
  34.5 189.3 %copy-start.59 = (f32[768]{0:T(1024)}, f32[768]{0:T(1024)S(1)}, u32[]{:S(2)}) copy-start(f32[768]{0:T(1024)S(1)} %get-tuple-element.220) | copy-start | bytes 9220
  34.5 288.7 %copy-start.42 = (f32[768]{0:T(1024)}, f32[768]{0:T(1024)S(1)}, u32[]{:S(2)}) copy-start(f32[768]{0:T(1024)S(1)} %get-tuple-element.221) | copy-start | bytes 9220
  152.4 3.1 copy-start.80
  160.2 2.6 copy-start.6
  178.3 4.7 copy-start
  178.3 4.7 copy-start.2
  178.4 4.7 copy-start.31
  178.4 4.7 copy-start.78
  183.0 3.5 copy-start.25
  186.5 37.3 %copy-start.13 = (f32[1024,768]{1,0:T(8,128)}, f32[1024,768]{1,0:T(8,128)S(1)}, u32[]{:S(2)}) copy-start(f32[1024,768]{1,0:T(8,128)S(1)} %get-tuple-element.291) | copy-start | bytes 9437188
  186.6 136.7 %copy-start.36 = (f32[1024]{0:T(1024)}, f32[1024]{0:T(1024)S(1)}, u32[]{:S(2)}) copy-start(f32[1024]{0:T(1024)S(1)} %broadcast_multiply_fusion.5) | copy-start | bytes 12292
  187.1 136.2 %copy-start.44 = (f32[1024]{0:T(1024)}, f32[1024]{0:T(1024)S(1)}, u32[]{:S(2)}) copy-start(f32[1024]{0:T(1024)S(1)} %add_rsqrt_fusion.1) | copy-start | bytes 12292
  187.1 36.8 %copy-start.61 = (f32[768]{0:T(1024)S(1)}, f32[768]{0:T(1024)}, u32[]{:S(2)}) copy-start(f32[768]{0:T(1024)} %get-tuple-element.219) | copy-start | bytes 9220
  223.8 10.0 %copy-start.82 = (bf16[1024,3072]{1,0:T(8,128)(2,1)}, bf16[1024,3072]{1,0:T(8,128)(2,1)S(1)}, u32[]{:S(2)}) copy-start(bf16[1024,3072]{1,0:T(8,128)(2,1)S(1)} %get-tuple-element.284) | copy-start | bytes 18874372
  234.3 3.4 copy-start.35
  234.4 3.5 copy-start.70
  234.4 3.7 copy-start.65
  234.4 3.9 copy-start.69
  234.4 4.5 copy-start.75
  236.2 47.9 %copy-start.40 = (bf16[2,1,768]{2,1,0:T(2,128)(2,1)}, bf16[2,1,768]{2,1,0:T(2,128)(2,1)S(1)}, u32[]{:S(2)}) copy-start(bf16[2,1,768]{2,1,0:T(2,128)(2,1)S(1)} %slice.126) | copy-start | bytes 9220
  237.8 46.4 %copy-start.56 = (f32[2,768]{1,0:T(2,128)}, f32[2,768]{1,0:T(2,128)S(1)}, u32[]{:S(2)}) copy-start(f32[2,768]{1,0:T(2,128)S(1)} %fusion.91) | copy-start | bytes 18436
  239.0 45.2 %copy-start.66 = (f32[2,3]{1,0:T(2,128)}, f32[2,3]{1,0:T(2,128)S(1)}, u32[]{:S(2)}) copy-start(f32[2,3]{1,0:T(2,128)S(1)} %get-tuple-element.282) | copy-start | bytes 76
  279.5 4.7 copy-start.48
  281.8 2.8 copy-start.4
  284.7 4.3 copy-start.5
  293.4 19.4 %copy-start.14 = (f32[1024,768]{1,0:T(8,128)S(1)}, f32[1024,768]{1,0:T(8,128)}, u32[]{:S(2)}) copy-start(f32[1024,768]{1,0:T(8,128)} %copy-done.13) | copy-start | bytes 9437188
  332.9 4.0 copy-start.1
  332.9 4.0 copy-start.3
  332.9 4.0 copy-start.32
  332.9 4.0 copy-start.81
  336.9 3.1 copy-start.7
  336.9 3.1 copy-start.8
  347.4 7.2 %copy-start.19 = (bf16[2,512,12,64]{1,3,2,0:T(8,128)(2,1)S(1)}, bf16[2,512,12,64]{1,3,2,0:T(8,128)(2,1)}, u32[]{:S(2)}) copy-start(bf16[2,512,12,64]{1,3,2,0:T(8,128)(2,1)} %get-tuple-element.453) | copy-start | bytes 4718596 | tf_op jit(solution)/shard_map/while
  362.7 3.1 copy-start.7
  362.7 3.1 copy-start.8
  373.2 7.2 %copy-start.19 = (bf16[2,512,12,64]{1,3,2,0:T(8,128)(2,1)S(1)}, bf16[2,512,12,64]{1,3,2,0:T(8,128)(2,1)}, u32[]{:S(2)}) copy-start(bf16[2,512,12,64]{1,3,2,0:T(8,128)(2,1)} %get-tuple-element.453) | copy-start | bytes 4718596 | tf_op jit(solution)/shard_map/while
  388.9 3.6 copy-start.79
  401.7 6.8 slice-start
  404.2 4.2 copy-start.15
  404.3 4.2 copy-start.37
  404.3 4.2 copy-start.43
  404.3 4.2 copy-start.45
  404.3 4.2 copy-start.60
  404.3 4.2 slice-start.1
  406.8 9.6 %slice-start.2 = ((s8[6291456]{0:T(1024)(128)(4,1)}), s8[4194304]{0:T(1024)(128)(4,1)S(1)}, s32[]{:S(2)}) async-start(s8[6291456]{0:T(1024)(128)(4,1)} %bitcast.233), calls=%async_computation.8 | async-start | bytes 8388608
  408.5 7.8 %copy-start.23 = (f32[1024,768]{1,0:T(8,128)S(1)}, f32[1024,768]{1,0:T(8,128)}, u32[]{:S(2)}) copy-start(f32[1024,768]{1,0:T(8,128)} %get-tuple-element.274) | copy-start | bytes 9437188
  408.5 7.8 %slice-start.3 = ((s8[6291456]{0:T(1024)(128)(4,1)}), s8[2097152]{0:T(1024)(128)(4,1)S(1)}, s32[]{:S(2)}) async-start(s8[6291456]{0:T(1024)(128)(4,1)} %bitcast.233), calls=%async_computation.9 | async-start | bytes 4194304
  423.6 212.2 %reduce-scatter.7.cloned.1.call-start = ((), (), s32[]{:S(2)}) async-start(), calls=%async_computation.5 | async-start | bytes 208896
  427.6 247.5 %all-reduce.3.cloned.1.call-start = ((), (), s32[]{:S(2)}) async-start(), calls=%async_computation.4 | async-start | bytes 1916928 | tf_op jit(solution)/shard_map/psum | solution.py:329
  427.6 5.0 copy-start.29
  432.6 146.4 %copy-start.71 = (f32[3]{0:T(128)S(1)}, f32[3]{0:T(128)}, u32[]{:S(2)}) copy-start(f32[3]{0:T(128)} %param.31) | copy-start | bytes 40
  432.6 146.4 %copy-start.72 = (f32[3]{0:T(128)S(1)}, f32[3]{0:T(128)}, u32[]{:S(2)}) copy-start(f32[3]{0:T(128)} %param.32) | copy-start | bytes 40
  432.6 146.4 %copy-start.73 = (f32[3]{0:T(128)S(1)}, f32[3]{0:T(128)}, u32[]{:S(2)}) copy-start(f32[3]{0:T(128)} %param.33) | copy-start | bytes 40
  432.6 146.4 %copy-start.74 = (f32[3]{0:T(128)S(1)}, f32[3]{0:T(128)}, u32[]{:S(2)}) copy-start(f32[3]{0:T(128)} %get-tuple-element.265) | copy-start | bytes 40
  432.6 149.0 %copy-start.18 = (f32[1024,768]{1,0:T(8,128)S(1)}, f32[1024,768]{1,0:T(8,128)}, u32[]{:S(2)}) copy-start(f32[1024,768]{1,0:T(8,128)} %copy-done.16) | copy-start | bytes 9437188
  581.6 59.9 %copy-start.39 = (f32[16,48]{1,0:T(8,128)S(1)}, f32[16,48]{1,0:T(8,128)}, u32[]{:S(2)}) copy-start(f32[16,48]{1,0:T(8,128)} %param.28) | copy-start | bytes 9220
  581.6 59.9 %copy-start.54 = (f32[16,48]{1,0:T(8,128)S(1)}, f32[16,48]{1,0:T(8,128)}, u32[]{:S(2)}) copy-start(f32[16,48]{1,0:T(8,128)} %param.29) | copy-start | bytes 9220
  581.6 59.9 %copy-start.55 = (f32[16,48]{1,0:T(8,128)S(1)}, f32[16,48]{1,0:T(8,128)}, u32[]{:S(2)}) copy-start(f32[16,48]{1,0:T(8,128)} %param.30) | copy-start | bytes 9220
  (34 other events, 65.6 us)
Sparse Core Ops, SparseCore 0:
  10.9 120.6 all-gather.2
  423.6 155.3 reduce-scatter.4
  583.1 52.7 reduce-scatter.6
  638.0 37.0 all-reduce.2
where the time goes:
time: 698 us; the launch traced here: 690 us
  waiting for transfers between devices  316 us (45%)
  matrix products  188 us (27%)
  blocking collectives  67.7 us (10%)
  other arithmetic  51.2 us (7%)
  local copies, waits for them, and re-layouts  48.4 us (7%)
  between operations  17.7 us (3%)
    reduce_scatter x1, waiting for transfers between devices, on_device(): lax.psum_scatter(mat_grad.astype(jnp.bfloat16), 'fsdp', scatter_dimension...  142 us
    all_gather x1, waiting for transfers between devices, on_device(): lax.all_gather(mat_low, 'fsdp', axis=0, tiled=True)  93.3 us
    dot_general x8, matrix products, product_last(): lax.dot_general(first_arg, second_arg, (((1,), (1,)), ((), ())), preferre...  77.4 us
    unnamed x5, waiting for transfers between devices  47.9 us
    psum x1, blocking collectives, on_device(): lax.psum((ce_sum, jnp.sum(active), error_sum), ('dp', 'fsdp'))  39.1 us
    dot_general x8, matrix products, product(): return jnp.dot(first_arg, second_arg, preferred_element_type=jnp.float32)  36.4 us
    psum x1, waiting for transfers between devices, on_device(): lax.psum(mat_part.astype(jnp.bfloat16), 'dp').astype(jnp.float32)  33 us
    dot_general x8, matrix products, product_first(): lax.dot_general(first_arg, second_arg, (((0,), (0,)), ((), ())), preferre...  27.4 us
  transfers between devices with their start and end apart: 4, of which 4 were waited for; matrix products, arithmetic and copies ran while one was open for 4% of the time, Pallas kernels for 0%

commit v1 on v0

--- a/solution.py
+++ b/solution.py
@@ -18,6 +18,19 @@
 LN_EPS = 1e-12
 VEC_RATE = 0.5
 MASK_FILL = -1000000000.0
+
+
+def collect(x, axis, dim):
+    ways = lax.axis_size(axis)
+    up = [(d, (d + 1) % ways) for d in range(ways)]
+    down = [(d, (d - 1) % ways) for d in range(ways)]
+    earlier, later = ([x], [x])
+    for _ in range(ways // 2):
+        earlier.append(lax.ppermute(earlier[-1], axis, up))
+    for _ in range((ways - 1) // 2):
+        later.append(lax.ppermute(later[-1], axis, down))
+    line = jnp.concatenate([*earlier[::-1], *later[1:]], axis=dim)
+    return jnp.roll(line, (lax.axis_index(axis) - ways // 2) * x.shape[dim], axis=dim)
 
 
 def product(first_arg, second_arg):
@@ -177,7 +190,7 @@
     vec_low = vec_master.astype(jnp.bfloat16)
     matrices, vectors = (
         lax.all_gather(mat_low, "fsdp", axis=0, tiled=True),
-        lax.all_gather(vec_low, "fsdp", axis=1, tiled=True),
+        collect(vec_low, "fsdp", 1),
     )
     w_query, w_key, w_value, w_out, w_pool, w_inner, w_outer = split_matrices(matrices)
     (

time: 698 us -> 741 us (1.062)
  matrix products: 188 us -> 230 us
  starting transfers between devices: 0.16 us -> 29.4 us
  waiting for transfers between devices: 316 us -> 290 us
    all_gather x1, waiting for transfers between devices: 93.3 us -> 56.9 us  [on_device(): lax.all_gather(mat_low, 'fsdp', axis=0, tiled=True)]
    ppermute x0 -> x15, starting transfers between devices: none -> 29 us  [the longest x7 28.4 us: collect(): later.append(lax.ppermute(later[-1], axis, down))]
    dot_general x8, matrix products: 36.4 us -> 65 us  [product(): return jnp.dot(first_arg, second_arg, preferred_element_type=jnp.float32)]
    dot_general x8, matrix products: 27.4 us -> 41.9 us  [product_first(): lax.dot_general(first_arg, second_arg, (((0,), (0,)), ((), ())), preferre...]
    ppermute x0 -> x15, waiting for transfers between devices: none -> 11.3 us  [the longest x8 7.16 us: collect(): earlier.append(lax.ppermute(earlier[-1], axis, up))]
  transfers between devices with their start and end apart: 4 -> 19, of which waited for: 4 -> 12; matrix products, arithmetic and copies ran while one was open for 4% -> 4% of each run, Pallas kernels for 0% -> 0%
where the time goes in v1:
time: 741 us; the launch traced here: 733 us
  waiting for transfers between devices  290 us (39%)
  matrix products  230 us (31%)
  blocking collectives  62.4 us (8%)
  other arithmetic  51.6 us (7%)
  local copies, waits for them, and re-layouts  50.4 us (7%)
  starting transfers between devices  29.4 us (4%)
  between operations  17.9 us (2%)
    reduce_scatter x1, waiting for transfers between devices, on_device(): lax.psum_scatter(mat_grad.astype(jnp.bfloat16), 'fsdp', scatter_dimension...  141 us
    dot_general x8, matrix products, product_last(): lax.dot_general(first_arg, second_arg, (((1,), (1,)), ((), ())), preferre...  76.3 us
    dot_general x8, matrix products, product(): return jnp.dot(first_arg, second_arg, preferred_element_type=jnp.float32)  65 us
    all_gather x1, waiting for transfers between devices, on_device(): lax.all_gather(mat_low, 'fsdp', axis=0, tiled=True)  56.9 us
    unnamed x5, waiting for transfers between devices  48 us
    dot_general x8, matrix products, product_first(): lax.dot_general(first_arg, second_arg, (((0,), (0,)), ((), ())), preferre...  41.9 us
    psum x1, blocking collectives, on_device(): lax.psum((ce_sum, jnp.sum(active), error_sum), ('dp', 'fsdp'))  38.8 us
    psum x1, waiting for transfers between devices, on_device(): lax.psum(mat_part.astype(jnp.bfloat16), 'dp').astype(jnp.float32)  33 us
  transfers between devices with their start and end apart: 19, of which 12 were waited for; matrix products, arithmetic and copies ran while one was open for 4% of the time, Pallas kernels for 0%

profile of v1, /device:TPU:0, one launch (start us, length us, event | category | flops | bytes accessed | tf_op | source)
XLA Modules:
  0.0 732.9 jit_solution(4224035854852971348)
XLA Ops:
  7.2 2.7 convert_element_type.141
  10.5 5.0 collective-permute-start.8
  16.9 4.4 collective-permute-start.9
  22.5 3.3 copy_convert_fusion
  25.8 4.4 collective-permute-start.10
  31.6 4.6 collective-permute-start.11
  36.2 18.7 %all-gather = bf16[16,48,16]{1,2,0:T(8,128)(2,1)S(1)} all-gather(bf16[1,48,16]{1,2,0:T(8,128)(2,1)S(1)} %convert_bitcast_fusion), channel_id=1, replica_groups=mesh['dp'=2,'fsdp'=16] {'fsdp'}, dimensions={0}, use_global_device_ids=true | all-gather | bytes 26112 | tf_op jit(solution)/shard_map/all_gather | solution.py:241
  57.4 4.4 collective-permute-start.13
  63.1 4.6 collective-permute-start.14
  69.0 4.7 collective-permute-done.7
  75.2 56.9 %all-gather.3.cloned.1.call-done = bf16[9984,768]{1,0:T(8,128)(2,1)} async-done(((bf16[624,768]{1,0:T(8,128)(2,1)}), bf16[9984,768]{1,0:T(8,128)(2,1)}) %all-gather.3.cloned.1.call-update) | async-done | bytes 15335440 | tf_op jit(solution)/shard_map/all_gather | solution.py:192
  132.0 3.1 add_convert_fusion.4
  138.9 2.7 add_convert_fusion.3
  144.9 3.8 convolution_convert_fusion.2
  148.7 1.7 copy.114
  150.4 2.4 reshape.217
  152.8 1.7 copy.117
  155.9 22.9 %while.27 = (s32[]{:T(128)}, bf16[2,512,12,64]{1,3,2,0:T(8,128)(2,1)}, f32[2,12,512,1]{2,1,3,0:T(8,128)S(1)}, bf16[2,512,12,64]{1,3,2,0:T(8,128)(2,1)}, s32[2]{0...) while((s32[]{:T(128)}, ...), condition=%wide.region_3.4_spmd, body=%wide.region_0.3_spmd.sunk | while | flops 843442688 | bytes 47427716 | solution.py:216
  157.5 3.1 fusion.227
  160.7 2.6 fusion.228
  163.3 4.2 fusion.229
  168.7 3.1 fusion.227
  171.8 2.6 fusion.228
  174.5 4.2 fusion.229
  178.8 4.2 copy.118
  183.5 3.5 fusion.185
  187.6 34.7 %fusion.60 = (f32[1024,3072]{1,0:T(8,128)}, f32[1024,3072]{1,0:T(8,128)S(1)}) fusion(f32[3072]{0:T(1024)S(1)} %add.278, bf16[9984,768]{1,0:T(8,128)(2,1)} %all-gather.3.cloned.1.call-done, f32[1024,768]{1,0:T(8,128)S(1)} %get-tuple-element.291, f32[768]{0:T(1024)S(1)} %get-tuple-element.222, f32[768]{0:T(1024)S(1)} %get-tuple-element.223, ...), kind=kOutput, calls=%fused_computation.67 | convolution fusion | flops 5033951232 | bytes 33056768 | tf_op jit(solution)/shard_map/dot_general | solution.py:41
  222.4 38.5 %fusion.186 = (f32[1024]{0:T(1024)S(1)}, f32[1024,768]{1,0:T(8,128)S(1)}) fusion(f32[768]{0:T(1024)S(1)} %copy-done.67, bf16[9984,768]{1,0:T(8,128)(2,1)} %all-gather.3.cloned.1.call-done, f32[1024,3072]{1,0:T(8,128)S(1)} %get-tuple-element.297, f32[3072]{0:T(1024)S(1)} %copy-done.53, f32[768]{0:T(1024)S(1)} %get-tuple-element.222, ...), kind=kOutput, calls=%fused_computation.275 | convolution fusion | flops 5044960256 | bytes 23626752 | tf_op jit(solution)/shard_map/dot_general | solution.py:37
  266.8 38.8 %all-reduce = (f32[]{:T(128)}, f32[]{:T(128)}, f32[3]{0:T(128)}) all-reduce(f32[]{:T(128)} %get-tuple-element.230, f32[]{:T(128)} %get-tuple-element.229, f32[3]{0:T(128)S(1)} %get-tuple-element.283), channel_id=1, replica_groups=mesh['dp'=2,'fsdp'=16] {'dp','fsdp'}, use_global_device_ids=true, to_apply=%region_11.12 | all-reduce | flops 5 | bytes 40 | tf_op jit(solution)/shard_map/psum | solution.py:236
  307.6 2.3 fusion.107
  309.9 2.3 copy.121
  312.7 2.6 fusion.176
  317.2 4.2 convert_reduce_fusion.1
  321.4 19.5 %fusion.189 = (bf16[3072]{0:T(1024)(128)(2,1)}, bf16[1024,3072]{1,0:T(8,128)(2,1)}) fusion(f32[1024,3072]{1,0:T(8,128)} %get-tuple-element.296, bf16[9984,768]{1,0:T(8,128)(2,1)} %all-gather.3.cloned.1.call-done, f32[1024,768]{1,0:T(8,128)} %get-tuple-element.276, f32[1024,3072]{1,0:T(8,128)} %copy-done.88, f32[3072]{0:T(1024)S(1)} %add.278), kind=kOutput, calls=%fused_computation.278 | convolution fusion | flops 4882953216 | bytes 39340032 | tf_op jit(solution)/shard_map/dot_general | solution.py:41
  340.8 10.5 %multiply_reduce_fusion.1 = (bf16[768]{0:T(1024)(128)(2,1)}, f32[1024]{0:T(1024)S(1)}, f32[1024]{0:T(1024)S(1)}, bf16[768]{0:T(1024)(128)(2,1)}, f32[1024,768]{1,0:T(8,128)S(1)}) fusion(f32[1024,768]{1,0:T(8,128)S(1)} %copy-done.14, f32[1024]{0:T(1024)S(1)} %add_rsqrt_fusion.1, f32[1024]{0:T(1024)S(1)} %broadcast_multiply_fusion.5, ...), kind=kOutput, calls=%fused_computation.115 | convolution fusion | flops 4839698432 | bytes 20469760 | tf_op jit(solution)/shard_map/dot_general | solution.py:37
  351.3 2.1 convert_reduce_fusion
  355.1 2.7 convolution_convert_fusion.1
  365.2 51.8 %while.28 = (s32[]{:T(128)}, bf16[2,512,12,64]{1,3,2,0:T(8,128)(2,1)}, bf16[2,512,12,64]{1,3,2,0:T(8,128)(2,1)}, bf16[2,512,12,64]{1,3,2,0:T(8,128)(2,1)}, bf16[...) while((s32[]{:T(128)}, ...), condition=%wide.region_18.19_spmd, body=%wide.region_16.18_spmd.sunk | while | flops 2062412288 | bytes 140180784 | solution.py:288
  365.3 1.8 fusion.238
  368.4 7.3 multiply_reduce_fusion.9
  375.7 7.2 multiply_convert_fusion.10
  383.0 2.0 fusion.240
  387.3 3.8 fusion.241
  391.1 1.8 fusion.238
  394.2 7.3 multiply_reduce_fusion.9
  401.6 7.2 multiply_convert_fusion.10
  408.8 2.0 fusion.240
  413.1 3.8 fusion.241
  417.1 3.1 copy.128
  420.7 2.5 fusion.101
  427.4 2.5 fusion.103
  429.9 2.5 fusion.105
  432.5 2.4 fusion.99
  434.9 1.7 fusion.98
  436.7 8.0 %fusion.78 = bf16[9984,768]{1,0:T(8,128)(2,1)} fusion(bf16[9984,768]{1,0:T(8,128)(2,1)} %fusion.98, bf16[1024,3072]{1,0:T(8,128)(2,1)S(1)} %bitcast.229, f32[1024,768]{1,0:T(8,128)S(1)} %copy-done.15, f32[768]{0:T(1024)S(1)} %copy-done.64, f32[768]{0:T(1024)S(1)} %copy-done.66, f32[1024]{0:T(1024)S(1)} %copy-done.47, f32[1024]{0:T(1024)S(1)} %copy-done.40), kind=kOutput, calls=%fused_computation.103 | convolution fusion | flops 4838129664 | bytes 14170112 | tf_op jit(solution)/shard_map/dot_general | solution.py:47
  444.7 21.4 %fusion.80 = bf16[9984,768]{1,0:T(8,128)(2,1)} fusion(bf16[9984,768]{1,0:T(8,128)(2,1)} %fusion.78, f32[1024,3072]{1,0:T(8,128)} %get-tuple-element.296, f32[1024,3072]{1,0:T(8,128)} %copy-done.88, f32[3072]{0:T(1024)S(1)} %copy-done.52, f32[1024,768]{1,0:T(8,128)S(1)} %copy-done.23), kind=kOutput, calls=%fused_computation.105 | convolution fusion | flops 4847566848 | bytes 33042432 | tf_op jit(solution)/shard_map/dot_general | solution.py:47
  470.5 5.0 fusion.117
  475.6 4.8 fusion.114
  480.4 141.1 %reduce-scatter.5.cloned.1.call-done = bf16[624,768]{1,0:T(8,128)(2,1)} async-done(((bf16[9984,768]{1,0:T(8,128)(2,1)}), bf16[624,768]{1,0:T(8,128)(2,1)}) %reduce-scatter.5.cloned.1.call-update) | async-done | bytes 958480 | tf_op jit(solution)/shard_map/reduce_scatter | solution.py:334
  624.1 6.3 add_convert_fusion.1
  630.4 47.9 %reduce-scatter.7.cloned.1.call-done = bf16[48,16]{1,0:T(8,128)(2,1)} async-done(((bf16[768,16]{1,0:T(8,128)(2,1)}), bf16[48,16]{1,0:T(8,128)(2,1)}) %reduce-scatter.7.cloned.1.call-update) | async-done | bytes 1552
  679.1 4.9 psum.38
  684.7 33.0 %all-reduce.3.cloned.1.call-done = bf16[624,768]{1,0:T(8,128)(2,1)} async-done(((bf16[624,768]{1,0:T(8,128)(2,1)}), bf16[624,768]{1,0:T(8,128)(2,1)}) %all-reduce.3.cloned.1.call-update) | async-done | bytes 958480 | tf_op jit(solution)/shard_map/psum | solution.py:342
  717.7 7.2 fusion.181
  (316 shorter events, 60.5 us)
Async XLA Ops:
  7.2 15.3 %copy-start.30 = (bf16[2,512,768]{2,1,0:T(8,128)(2,1)S(1)}, bf16[2,512,768]{2,1,0:T(8,128)(2,1)}, u32[]{:S(2)}) copy-start(bf16[2,512,768]{2,1,0:T(8,128)(2,1)} %param.21) | copy-start | bytes 4718596
  7.2 124.8 %all-gather.3.cloned.1.call-start = ((), (), s32[]{:S(2)}) async-start(), calls=%async_computation.2 | async-start | bytes 16293888 | tf_op jit(solution)/shard_map/all_gather | solution.py:192
  9.9 51.9 %copy-start.76 = (s32[2]{0:T(128)S(1)}, s32[2]{0:T(128)}, u32[]{:S(2)}) copy-start(s32[2]{0:T(128)} %param.24) | copy-start | bytes 28
  9.9 611.5 %reduce-scatter.5.cloned.1.call-start = ((), (), s32[]{:S(2)}) async-start(), calls=%async_computation.3 | async-start | bytes 16293888 | tf_op jit(solution)/shard_map/reduce_scatter | solution.py:334
  10.0 6.8 collective-permute-start
  10.5 6.4 collective-permute-start.8
  16.8 5.7 collective-permute-start.1
  16.9 8.9 %collective-permute-start.9 = (bf16[16,48]{1,0:T(8,128)(2,1)S(1)}, bf16[16,48]{1,0:T(8,128)(2,1)S(1)}, u32[]{:S(2)}, u32[]{:S(2)}) collective-permute-start(bf16[16,48]{1,0:T(8,128)(2,1)S(1)} %collective-permute-done.8), channel_id=1, source_target_pairs={{0,15},{1,0},{2,1},{3,2},{4,3},{5,4},{6,5},{7,6},{8,7},{9,8},{10,9... | collective-permute-start | bytes 4616 | tf_op jit(solution)/shard_map/ppermute | solution.py:31
  22.5 7.8 %collective-permute-start.2 = (bf16[16,48]{1,0:T(8,128)(2,1)S(1)}, bf16[16,48]{1,0:T(8,128)(2,1)S(1)}, u32[]{:S(2)}, u32[]{:S(2)}) collective-permute-start(bf16[16,48]{1,0:T(8,128)(2,1)S(1)} %collective-permute-done.1), channel_id=1, source_target_pairs={{0,1},{1,2},{2,3},{3,4},{4,5},{5,6},{6,7},{7,8},{8,9},{9,10},{10,1... | collective-permute-start | bytes 4616 | tf_op jit(solution)/shard_map/ppermute | solution.py:29
  25.8 5.8 collective-permute-start.10
  30.3 5.9 collective-permute-start.3
  31.6 23.5 %collective-permute-start.11 = (bf16[16,48]{1,0:T(8,128)(2,1)S(1)}, bf16[16,48]{1,0:T(8,128)(2,1)S(1)}, u32[]{:S(2)}, u32[]{:S(2)}) collective-permute-start(bf16[16,48]{1,0:T(8,128)(2,1)S(1)} %collective-permute-done.10), channel_id=1, source_target_pairs={{0,15},{1,0},{2,1},{3,2},{4,3},{5,4},{6,5},{7,6},{8,7},{9,8},{10,9... | collective-permute-start | bytes 4616 | tf_op jit(solution)/shard_map/ppermute | solution.py:31
  36.2 19.9 %collective-permute-start.4 = (bf16[16,48]{1,0:T(8,128)(2,1)S(1)}, bf16[16,48]{1,0:T(8,128)(2,1)S(1)}, u32[]{:S(2)}, u32[]{:S(2)}) collective-permute-start(bf16[16,48]{1,0:T(8,128)(2,1)S(1)} %collective-permute-done.3), channel_id=1, source_target_pairs={{0,1},{1,2},{2,3},{3,4},{4,5},{5,6},{6,7},{7,8},{8,9},{9,10},{10,1... | collective-permute-start | bytes 4616 | tf_op jit(solution)/shard_map/ppermute | solution.py:29
  55.0 14.0 %copy-start.34 = (bf16[768,16]{0,1:T(8,128)(2,1)}, bf16[768,16]{0,1:T(8,128)(2,1)S(1)}, u32[]{:S(2)}) copy-start(bf16[768,16]{0,1:T(8,128)(2,1)S(1)} %reshape.229) | copy-start | bytes 73732
  55.0 2.3 collective-permute-start.12
  56.1 5.7 collective-permute-start.5
  57.4 5.7 collective-permute-start.13
  61.8 5.9 collective-permute-start.6
  63.1 5.9 collective-permute-start.14
  67.7 5.9 collective-permute-start.7
  68.4 253.0 %copy-start.51 = (f32[3072]{0:T(1024)}, f32[3072]{0:T(1024)S(1)}, u32[]{:S(2)}) copy-start(f32[3072]{0:T(1024)S(1)} %add.278) | copy-start | bytes 36868
  73.8 58.2 %copy-start.33 = (bf16[16,1536]{1,0:T(8,128)(2,1)}, bf16[16,1536]{1,0:T(8,128)(2,1)S(1)}, u32[]{:S(2)}) copy-start(bf16[16,1536]{1,0:T(8,128)(2,1)S(1)} %concatenate.16) | copy-start | bytes 147460
  75.2 147.2 %copy-start.63 = (f32[768]{0:T(1024)}, f32[768]{0:T(1024)S(1)}, u32[]{:S(2)}) copy-start(f32[768]{0:T(1024)S(1)} %get-tuple-element.222) | copy-start | bytes 9220
  75.2 147.2 %copy-start.65 = (f32[768]{0:T(1024)}, f32[768]{0:T(1024)S(1)}, u32[]{:S(2)}) copy-start(f32[768]{0:T(1024)S(1)} %get-tuple-element.223) | copy-start | bytes 9220
  178.8 4.7 copy-start
  178.8 4.7 copy-start.2
  178.8 4.7 copy-start.31
  178.8 4.7 copy-start.84
  187.0 35.3 %copy-start.13 = (f32[1024,768]{1,0:T(8,128)}, f32[1024,768]{1,0:T(8,128)S(1)}, u32[]{:S(2)}) copy-start(f32[1024,768]{1,0:T(8,128)S(1)} %get-tuple-element.291) | copy-start | bytes 9437188
  187.1 164.2 %copy-start.39 = (f32[1024]{0:T(1024)}, f32[1024]{0:T(1024)S(1)}, u32[]{:S(2)}) copy-start(f32[1024]{0:T(1024)S(1)} %broadcast_multiply_fusion.5) | copy-start | bytes 12292
  187.6 163.7 %copy-start.46 = (f32[1024]{0:T(1024)}, f32[1024]{0:T(1024)S(1)}, u32[]{:S(2)}) copy-start(f32[1024]{0:T(1024)S(1)} %add_rsqrt_fusion.1) | copy-start | bytes 12292
  187.6 34.7 %copy-start.53 = (f32[3072]{0:T(1024)S(1)}, f32[3072]{0:T(1024)}, u32[]{:S(2)}) copy-start(f32[3072]{0:T(1024)} %add.260) | copy-start | bytes 36868
  187.6 34.7 %copy-start.67 = (f32[768]{0:T(1024)S(1)}, f32[768]{0:T(1024)}, u32[]{:S(2)}) copy-start(f32[768]{0:T(1024)} %get-tuple-element.221) | copy-start | bytes 9220
  222.3 38.5 %copy-start.88 = (f32[1024,3072]{1,0:T(8,128)}, f32[1024,3072]{1,0:T(8,128)S(1)}, u32[]{:S(2)}) copy-start(f32[1024,3072]{1,0:T(8,128)S(1)} %get-tuple-element.297) | copy-start | bytes 37748740
  261.4 4.5 copy-start.73
  261.4 4.7 copy-start.77
  261.4 5.3 copy-start.81
  261.4 44.2 %copy-start.35 = (bf16[768,16]{0,1:T(8,128)(2,1)S(1)}, bf16[768,16]{0,1:T(8,128)(2,1)}, u32[]{:S(2)}) copy-start(bf16[768,16]{0,1:T(8,128)(2,1)} %copy-done.34) | copy-start | bytes 73732
  263.3 48.9 %copy-start.43 = (bf16[2,1,768]{2,1,0:T(2,128)(2,1)}, bf16[2,1,768]{2,1,0:T(2,128)(2,1)S(1)}, u32[]{:S(2)}) copy-start(bf16[2,1,768]{2,1,0:T(2,128)(2,1)S(1)} %slice.138) | copy-start | bytes 9220
  264.8 47.4 %copy-start.41 = (f32[2,768]{1,0:T(2,128)}, f32[2,768]{1,0:T(2,128)S(1)}, u32[]{:S(2)}) copy-start(f32[2,768]{1,0:T(2,128)S(1)} %fusion.108) | copy-start | bytes 18436
  266.8 45.4 %copy-start.74 = (f32[2,3]{1,0:T(2,128)}, f32[2,3]{1,0:T(2,128)S(1)}, u32[]{:S(2)}) copy-start(f32[2,3]{1,0:T(2,128)S(1)} %get-tuple-element.284) | copy-start | bytes 76
  312.2 4.8 copy-start.5
  321.4 19.5 %copy-start.14 = (f32[1024,768]{1,0:T(8,128)S(1)}, f32[1024,768]{1,0:T(8,128)}, u32[]{:S(2)}) copy-start(f32[1024,768]{1,0:T(8,128)} %copy-done.13) | copy-start | bytes 9437188
  321.4 19.5 %copy-start.45 = (f32[768]{0:T(1024)S(1)}, f32[768]{0:T(1024)}, u32[]{:S(2)}) copy-start(f32[768]{0:T(1024)} %get-tuple-element.216) | copy-start | bytes 9220
  375.7 7.2 copy-start.19
  401.6 7.2 copy-start.19
  429.8 6.8 slice-start
  432.4 4.3 copy-start.15
  432.4 4.3 copy-start.40
  432.4 4.2 copy-start.47
  432.4 4.2 copy-start.64
  436.7 8.0 %copy-start.23 = (f32[1024,768]{1,0:T(8,128)S(1)}, f32[1024,768]{1,0:T(8,128)}, u32[]{:S(2)}) copy-start(f32[1024,768]{1,0:T(8,128)} %get-tuple-element.276) | copy-start | bytes 9437188
  436.7 8.0 %copy-start.52 = (f32[3072]{0:T(1024)S(1)}, f32[3072]{0:T(1024)}, u32[]{:S(2)}) copy-start(f32[3072]{0:T(1024)} %copy-done.51) | copy-start | bytes 36868
  466.2 212.1 %reduce-scatter.7.cloned.1.call-start = ((), (), s32[]{:S(2)}) async-start(), calls=%async_computation.5 | async-start | bytes 208896
  470.2 247.4 %all-reduce.3.cloned.1.call-start = ((), (), s32[]{:S(2)}) async-start(), calls=%async_computation.4 | async-start | bytes 1916928 | tf_op jit(solution)/shard_map/psum | solution.py:342
  470.5 5.1 copy-start.29
  475.6 145.9 %copy-start.72 = (f32[3]{0:T(128)S(1)}, f32[3]{0:T(128)}, u32[]{:S(2)}) copy-start(f32[3]{0:T(128)} %param.31) | copy-start | bytes 40
  475.6 146.0 %copy-start.78 = (f32[3]{0:T(128)S(1)}, f32[3]{0:T(128)}, u32[]{:S(2)}) copy-start(f32[3]{0:T(128)} %param.32) | copy-start | bytes 40
  475.6 146.0 %copy-start.79 = (f32[3]{0:T(128)S(1)}, f32[3]{0:T(128)}, u32[]{:S(2)}) copy-start(f32[3]{0:T(128)} %param.33) | copy-start | bytes 40
  475.6 146.0 %copy-start.80 = (f32[3]{0:T(128)S(1)}, f32[3]{0:T(128)}, u32[]{:S(2)}) copy-start(f32[3]{0:T(128)} %get-tuple-element.267) | copy-start | bytes 40
  475.6 148.5 %copy-start.18 = (f32[1024,768]{1,0:T(8,128)S(1)}, f32[1024,768]{1,0:T(8,128)}, u32[]{:S(2)}) copy-start(f32[1024,768]{1,0:T(8,128)} %copy-done.16) | copy-start | bytes 9437188
  624.1 60.0 %copy-start.37 = (f32[16,48]{1,0:T(8,128)S(1)}, f32[16,48]{1,0:T(8,128)}, u32[]{:S(2)}) copy-start(f32[16,48]{1,0:T(8,128)} %param.28) | copy-start | bytes 9220
  624.1 60.0 %copy-start.60 = (f32[16,48]{1,0:T(8,128)S(1)}, f32[16,48]{1,0:T(8,128)}, u32[]{:S(2)}) copy-start(f32[16,48]{1,0:T(8,128)} %param.29) | copy-start | bytes 9220
  624.1 60.0 %copy-start.61 = (f32[16,48]{1,0:T(8,128)S(1)}, f32[16,48]{1,0:T(8,128)}, u32[]{:S(2)}) copy-start(f32[16,48]{1,0:T(8,128)} %param.30) | copy-start | bytes 9220
  (53 other events, 127.8 us)
Sparse Core Ops, SparseCore 0:
  10.9 121.0 all-gather.2
  466.2 155.1 reduce-scatter.4
  625.6 52.7 reduce-scatter.6
  680.5 37.1 all-reduce.2
